TPU v7x, 256 devices: a whole 4x4x8 slice. The times are simulated.
256 devices in a mesh: feat: 32 (over y, z), dp: 8 (over x, core).
Axes of the slice: x: 4, y: 4, z: 8, core: 2. Of those that a mesh axis runs over, the one named last changes fastest.
Arguments:
- query_grads: bfloat16 [512, 131072], P(('dp', 'feat')), may hold values from -52 to 52
- build_grads: bfloat16 [1024, 131072], P('dp', 'feat'), may hold values from -52 to 52
- scored_grads: bfloat16 [4096, 131072], P('dp', 'feat'), may hold values from -52 to 52
Outputs:
- scores: float32 [4096, 512], P(('dp', 'feat'))
All inputs are finite; a program needn't handle non-finite values.
Results may differ from a plain program's by a relative error of at most 0.0049.
Values may be sent and summed in bfloat16 or wider, within the bound.
No kernel may reach another device: no remote copies, remote signals or barrier semaphores. Data moves between devices by JAX's collectives and lax.ppermute only.
A program may use at most 128 MiB of HBM per device.

v0:
```python
import functools
import jax
import jax.numpy as jnp
from jax import lax
from jax.sharding import Mesh
from jax.sharding import PartitionSpec as P

FEAT = 131072
FEAT_AXES = ("feat_0", "feat_1")
DP = ("dp_0", "dp_1")
FEAT_DP = ("feat_0", "feat_1", "dp_0", "dp_1")
DP_FEAT = ("dp_0", "dp_1", "feat_0", "feat_1")


def one_axis_at_a_time(shard, axes):
    return functools.reduce(lax.psum, axes, shard)


def sent_to_all(shard, axis):
    size = lax.axis_size(axis)
    return lax.all_to_all(
        jnp.broadcast_to(shard[None], (size, *shard.shape)), axis, 0, 0, tiled=True
    )


def taken_together(shard, axis):
    everything = sent_to_all(shard, axis)
    return jnp.sum(everything, axis=0)


def split_up(shard, dim, size):
    before, after = (shard.shape[:dim], shard.shape[dim + 1 :])
    return jnp.moveaxis(shard.reshape(*before, size, -1, *after), dim, 0)


def sent_and_summed(shard, axis, dim):
    size = lax.axis_size(axis)
    blocks = lax.all_to_all(split_up(shard, dim, size), axis, 0, 0, tiled=True)
    return jnp.sum(blocks, axis=0)


def contract_last(left, right):
    return lax.dot_general(
        left, right, (((1,), (1,)), ((), ())), preferred_element_type=jnp.float32
    )


def on_device(query_grads, build_grads, scored_grads):
    q_local = lax.all_to_all(query_grads, FEAT_AXES, split_axis=1, concat_axis=0, tiled=True)
    gathered = lax.all_gather(build_grads, DP, axis=0, tiled=True)
    build_count = gathered.shape[0]
    cross_part = contract_last(gathered, q_local)
    gram_part = contract_last(gathered, gathered)
    gram_matrix, cross_sums = lax.psum((gram_part, cross_part), FEAT_AXES)
    build_wide = build_grads.astype(jnp.float32)
    square_total = one_axis_at_a_time(jnp.sum(build_wide * build_wide), FEAT_DP)
    damping = 0.1 * square_total / (build_count * FEAT) + 1e-06
    gram_matrix = gram_matrix + build_count * damping * jnp.eye(build_count, dtype=jnp.float32)
    factor = jnp.linalg.cholesky(gram_matrix)
    solved = jax.scipy.linalg.cho_solve((factor, True), cross_sums)
    solved_half = solved.astype(jnp.bfloat16)
    query_wide = q_local.astype(jnp.float32)
    removed = lax.dot_general(
        solved_half, gathered, (((0,), (0,)), ((), ())), preferred_element_type=jnp.float32
    )
    precond = (query_wide - removed) / damping
    self_score = taken_together(jnp.sum(query_wide * precond, axis=1), FEAT_AXES)
    normed = (precond / jnp.sqrt(self_score)[:, None]).astype(jnp.bfloat16)
    partial_value = contract_last(scored_grads, lax.all_gather(normed, DP, axis=0, tiled=True))
    return sent_and_summed(partial_value, FEAT_AXES, 0)


def solution(mesh):
    torus = Mesh(mesh.devices.reshape(4, 8, 4, 2), ("feat_0", "feat_1", "dp_0", "dp_1"))
    in_specs = (P(DP_FEAT, None), P(DP, FEAT_AXES), P(DP, FEAT_AXES))
    out_specs = P(DP_FEAT, None)
    return jax.shard_map(
        on_device, mesh=torus, in_specs=in_specs, out_specs=out_specs, check_vma=False
    )
```

profile of v0, /device:TPU:32, one launch (start us, length us, event | category | flops | bytes accessed | tf_op | source)
XLA Modules:
  0.0 705.6 jit_solution(6234472942404162147)
XLA Ops:
  7.3 29.0 %all_to_all.30 = bf16[2,32,4096]{2,0,1:T(2,128)(2,1)S(1)} all-to-all(bf16[2,32,4096]{2,0,1:T(2,128)(2,1)} %bitcast.141), channel_id=1, replica_groups=mesh['feat_0'=4,'feat_1'=8,'dp_0'=4,'dp_1'=2] {'feat_0','feat_1'}, dimensions={1} | all-to-all | bytes 1048576 | tf_op jit(solution)/shard_map/all_to_all | solution.py:49
  36.5 27.5 %all-gather.3.cloned.1.call-done = bf16[1024,4096]{1,0:T(8,128)(2,1)} async-done(((bf16[128,4096]{1,0:T(8,128)(2,1)}), bf16[1024,4096]{1,0:T(8,128)(2,1)}) %all-gather.3.cloned.1.call-update) | async-done | bytes 8388624 | tf_op jit(solution)/shard_map/all_gather | solution.py:50
  64.0 16.0 %fusion.97 = f32[1024,1024]{0,1:T(8,128)} fusion(bf16[1024,4096]{1,0:T(8,128)(2,1)} %all-gather.3.cloned.1.call-done), kind=kOutput, calls=%fused_computation.222 | convolution fusion | flops 8589934592 | bytes 12582912 | tf_op jit(solution)/shard_map/dot_general | solution.py:43
  80.0 3.4 fusion.98
  85.7 11.1 %psum.43 = f32[]{:T(128)} all-reduce(f32[]{:T(128)} %multiply_reduce_fusion), channel_id=1, replica_groups=mesh['feat_0'=4,'feat_1'=8,'dp_0'=4,'dp_1'=2] {'feat_0'}, use_global_device_ids=true, to_apply=%region_2.0 | all-reduce | flops 1 | bytes 8 | tf_op jit(solution)/shard_map/psum | solution.py:16
  96.8 16.9 %psum.44 = f32[]{:T(128)} all-reduce(f32[]{:T(128)} %psum.43), channel_id=1, replica_groups=mesh['feat_0'=4,'feat_1'=8,'dp_0'=4,'dp_1'=2] {'feat_1'}, use_global_device_ids=true, to_apply=%region_3.0 | all-reduce | flops 1 | bytes 8 | tf_op jit(solution)/shard_map/psum | solution.py:16
  113.7 9.3 %psum.45 = f32[]{:T(128)} all-reduce(f32[]{:T(128)} %psum.44), channel_id=1, replica_groups=mesh['feat_0'=4,'feat_1'=8,'dp_0'=4,'dp_1'=2] {'dp_0'}, use_global_device_ids=true, to_apply=%region_4.0 | all-reduce | flops 1 | bytes 8 | tf_op jit(solution)/shard_map/psum | solution.py:16
  123.0 3.1 psum.46
  126.7 122.8 %all-reduce.4.cloned.1.call-done = (f32[1024,1024]{0,1:T(8,128)}, f32[1024,64]{0,1:T(8,128)}) async-done(((f32[1024,1024]{0,1:T(8,128)}, f32[1024,64]{0,1:T(8,128)}), (f32[1024,1024]{0,1:T(8,128)}, f32[1024,64]{0,1:T(8,128)})) %all-reduce.4.cloned.1.call-update) | async-done | bytes 4456464 | tf_op jit(solution)/shard_map/psum | solution.py:54
  249.5 4.8 select_add_fusion
  254.3 5.8 copy.44
  260.1 4.5 fusion
  264.6 2.0 copy-done.2
  266.6 11.7 %cholesky.222 = f32[128,128]{1,0:T(8,128)S(1)} custom-call(f32[128,128]{1,0:T(8,128)S(1)} %cholesky.577), custom_call_target="Cholesky" | custom-call | tf_op jit(solution)/shard_map/jit(cholesky)/cholesky | solution.py:59
  278.4 9.8 %custom-call.66 = f32[1,128,128]{1,2,0:T(8,128)S(1)} custom-call(f32[1,128,128]{2,1,0:T(8,128)S(1)} %get-tuple-element.50), custom_call_target="InvertDiagBlocksLowerTriangular" | custom-call | tf_op jit(solution)/shard_map/jit(cholesky)/cholesky | solution.py:59
  288.2 1.5 fusion.11
  290.0 1.6 convolution_subtract_fusion.1
  291.5 11.7 %cholesky.243 = f32[128,128]{1,0:T(8,128)S(1)} custom-call(f32[128,128]{1,0:T(8,128)S(1)} %cholesky.581), custom_call_target="Cholesky" | custom-call | tf_op jit(solution)/shard_map/jit(cholesky)/cholesky | solution.py:59
  303.5 9.8 %custom-call.67 = f32[1,128,128]{1,2,0:T(8,128)S(1)} custom-call(f32[1,128,128]{2,1,0:T(8,128)S(1)} %get-tuple-element.48), custom_call_target="InvertDiagBlocksLowerTriangular" | custom-call | tf_op jit(solution)/shard_map/jit(cholesky)/cholesky | solution.py:59
  314.5 1.9 copy-done.1
  316.4 2.4 convolution_subtract_fusion.2
  318.9 11.7 %cholesky.466 = f32[128,128]{1,0:T(8,128)S(1)} custom-call(f32[128,128]{1,0:T(8,128)S(1)} %cholesky.586), custom_call_target="Cholesky" | custom-call | tf_op jit(solution)/shard_map/jit(cholesky)/cholesky | solution.py:59
  331.3 9.8 %custom-call.68 = f32[1,128,128]{1,2,0:T(8,128)S(1)} custom-call(f32[1,128,128]{2,1,0:T(8,128)S(1)} %get-tuple-element.46), custom_call_target="InvertDiagBlocksLowerTriangular" | custom-call | tf_op jit(solution)/shard_map/jit(cholesky)/cholesky | solution.py:59
  341.2 1.2 convolution_dynamic-update-slice_fusion.1
  342.4 3.3 convolution_subtract_fusion.3
  345.7 11.7 %cholesky.485 = f32[128,128]{1,0:T(8,128)S(1)} custom-call(f32[128,128]{1,0:T(8,128)S(1)} %cholesky.591), custom_call_target="Cholesky" | custom-call | tf_op jit(solution)/shard_map/jit(cholesky)/cholesky | solution.py:59
  358.2 9.8 %custom-call.69 = f32[1,128,128]{1,2,0:T(8,128)S(1)} custom-call(f32[1,128,128]{2,1,0:T(8,128)S(1)} %get-tuple-element.44), custom_call_target="InvertDiagBlocksLowerTriangular" | custom-call | tf_op jit(solution)/shard_map/jit(cholesky)/cholesky | solution.py:59
  369.2 3.2 convolution_subtract_fusion.4
  372.3 12.1 %cholesky.504 = f32[128,128]{1,0:T(8,128)S(1)} custom-call(f32[128,128]{1,0:T(8,128)S(1)} %cholesky.596), custom_call_target="Cholesky" | custom-call | tf_op jit(solution)/shard_map/jit(cholesky)/cholesky | solution.py:59
  385.2 9.8 %custom-call.70 = f32[1,128,128]{1,2,0:T(8,128)S(1)} custom-call(f32[1,128,128]{2,1,0:T(8,128)S(1)} %get-tuple-element.42), custom_call_target="InvertDiagBlocksLowerTriangular" | custom-call | tf_op jit(solution)/shard_map/jit(cholesky)/cholesky | solution.py:59
  396.2 3.1 convolution_subtract_fusion.5
  399.3 11.7 %cholesky.524 = f32[128,128]{1,0:T(8,128)S(1)} custom-call(f32[128,128]{1,0:T(8,128)S(1)} %cholesky.601), custom_call_target="Cholesky" | custom-call | tf_op jit(solution)/shard_map/jit(cholesky)/cholesky | solution.py:59
  411.8 9.8 %custom-call.71 = f32[1,128,128]{1,2,0:T(8,128)S(1)} custom-call(f32[1,128,128]{2,1,0:T(8,128)S(1)} %get-tuple-element.40), custom_call_target="InvertDiagBlocksLowerTriangular" | custom-call | tf_op jit(solution)/shard_map/jit(cholesky)/cholesky | solution.py:59
  422.6 2.8 convolution_subtract_fusion.6
  425.4 11.7 %cholesky.544 = f32[128,128]{1,0:T(8,128)S(1)} custom-call(f32[128,128]{1,0:T(8,128)S(1)} %cholesky.606), custom_call_target="Cholesky" | custom-call | tf_op jit(solution)/shard_map/jit(cholesky)/cholesky | solution.py:59
  437.9 9.8 %custom-call.72 = f32[1,128,128]{1,2,0:T(8,128)S(1)} custom-call(f32[1,128,128]{2,1,0:T(8,128)S(1)} %get-tuple-element.38), custom_call_target="InvertDiagBlocksLowerTriangular" | custom-call | tf_op jit(solution)/shard_map/jit(cholesky)/cholesky | solution.py:59
  448.6 2.1 convolution_subtract_fusion.7
  450.7 11.7 %cholesky.562 = f32[128,128]{1,0:T(8,128)S(1)} custom-call(f32[128,128]{1,0:T(8,128)S(1)} %convolution_subtract_fusion.7), custom_call_target="Cholesky" | custom-call | tf_op jit(solution)/shard_map/jit(cholesky)/cholesky | solution.py:59
  472.7 4.9 select_select_fusion
  477.6 24.0 %while.1 = (s32[]{:T(128)}, f32[1024,1024]{0,1:T(8,128)}, s32[8,2]{0,1:T(2,128)S(1)}, f32[8,128,128]{2,1,0:T(8,128)S(1)}, s32[]{:T(128)}) while((s32[]{:T(128)}, f32[1024,1024]{0,1:T(8,128)}, s32[8,2]{0,1:T(2,128)S(1)}, f32[8,128,128]{2,1,0:T(8,128)S(1)}, s32[]{:T(128)}) %tuple.53), condition=%wide.while_cond, body=%wide.while_body.sunk | while | flops 2 | bytes 393329 | solution.py:60
  478.2 2.3 dynamic-slice.7
  481.2 2.3 dynamic-slice.7
  484.2 2.3 dynamic-slice.7
  487.2 2.3 dynamic-slice.7
  490.2 2.3 dynamic-slice.7
  493.2 2.3 dynamic-slice.7
  496.2 2.3 dynamic-slice.7
  499.2 2.2 dynamic-slice.7
  501.5 78.8 %custom-call.73 = f32[8,128,128]{1,2,0:T(8,128)S(1)} custom-call(f32[8,128,128]{2,1,0:T(8,128)S(1)} %get-tuple-element.12), custom_call_target="InvertDiagBlocksLowerTriangular" | custom-call | tf_op jit(solution)/shard_map/jit(_cho_solve)/triangular_solve | solution.py:60
  583.1 1.2 convolution_subtract_fusion.13
  584.5 1.2 convolution_subtract_fusion.21
  585.9 1.3 convolution_subtract_fusion.20
  587.4 1.4 convolution_subtract_fusion.19
  589.0 1.4 convolution_subtract_fusion.12
  593.6 1.3 convolution_subtract_fusion.9
  595.2 1.4 convolution_subtract_fusion.18
  596.9 1.5 convolution_subtract_fusion.17
  598.6 1.5 convolution_subtract_fusion.16
  600.5 1.7 convolution_subtract_fusion.8
  602.5 5.2 fusion.2
  607.7 14.9 %all_to_all.31 = f32[32,1,64]{2,1,0:T(1,128)S(1)} all-to-all(f32[32,1,64]{2,1,0:T(1,128)S(1)} %broadcast_in_dim.4), channel_id=1, replica_groups=mesh['feat_0'=4,'feat_1'=8,'dp_0'=4,'dp_1'=2] {'feat_0','feat_1'}, dimensions={0} | all-to-all | bytes 16384 | tf_op jit(solution)/shard_map/all_to_all | solution.py:21
  623.6 30.1 %all-gather.5.cloned.1.call-done = bf16[512,4096]{1,0:T(8,128)(2,1)} async-done(((bf16[64,4096]{1,0:T(8,128)(2,1)}), bf16[512,4096]{1,0:T(8,128)(2,1)}) %all-gather.5.cloned.1.call-update) | async-done | bytes 4194320 | tf_op jit(solution)/shard_map/all_gather | solution.py:69
  653.7 5.8 fusion.99
  659.6 38.6 %all_to_all.32 = f32[32,16,512]{2,1,0:T(8,128)S(1)} all-to-all(f32[32,16,512]{2,1,0:T(8,128)S(1)} %bitcast.140), channel_id=1, replica_groups=mesh['feat_0'=4,'feat_1'=8,'dp_0'=4,'dp_1'=2] {'feat_0','feat_1'}, dimensions={0} | all-to-all | bytes 2097152 | tf_op jit(solution)/shard_map/all_to_all | solution.py:38
  (143 shorter events, 33.8 us)
Async XLA Ops:
  6.5 57.5 %all-gather.3.cloned.1.call-start = ((), (), s32[]{:S(2)}) async-start(), calls=%async_computation.3 | async-start | bytes 9437184 | tf_op jit(solution)/shard_map/all_gather | solution.py:50
  7.3 242.2 %all-reduce.4.cloned.1.call-start = ((), (), s32[]{:S(2)}) async-start(), calls=%async_computation.5 | async-start | bytes 8912896 | tf_op jit(solution)/shard_map/psum | solution.py:54
  64.0 16.0 %copy-start = (bf16[1024,4096]{1,0:T(8,128)(2,1)S(1)}, bf16[1024,4096]{1,0:T(8,128)(2,1)}, u32[]{:S(2)}) copy-start(bf16[1024,4096]{1,0:T(8,128)(2,1)} %all-gather.3.cloned.1.call-done) | copy-start | bytes 25165828
  83.3 1.2 copy-start.3
  83.4 570.4 %all-gather.5.cloned.1.call-start = ((), (), s32[]{:S(2)}) async-start(), calls=%async_computation.4 | async-start | bytes 4718592 | tf_op jit(solution)/shard_map/all_gather | solution.py:69
  264.6 2.0 copy-start.2
  314.5 2.0 copy-start.1
  472.6 107.7 %copy-start.4 = (f32[1024,64]{0,1:T(8,128)S(1)}, f32[1024,64]{0,1:T(8,128)}, u32[]{:S(2)}) copy-start(f32[1024,64]{0,1:T(8,128)} %get-tuple-element.34) | copy-start | bytes 786436
Sparse Core Ops, SparseCore 0:
  9.2 54.7 all-gather.2
  83.5 165.9 all-reduce.3
  623.7 29.9 all-gather.4
where the time goes:
time: 713 us; the launch traced here: 706 us
  other arithmetic  263 us (37%)
  waiting for transfers between devices  181 us (25%)
  blocking collectives  123 us (17%)
  matrix products  77.9 us (11%)
  local copies, waits for them, and re-layouts  40.5 us (6%)
  between operations  19.6 us (3%)
    another operation x30, other arithmetic, on_device(): factor = jnp.linalg.cholesky(gram_matrix)  168 us
    psum x1, waiting for transfers between devices, on_device(): gram_matrix, cross_sums = lax.psum((gram_part, cross_part), FEAT_AXES)  123 us
    another operation x4, other arithmetic, on_device(): solved = jax.scipy.linalg.cho_solve((factor, True), cross_sums)  83.7 us
    psum x4, blocking collectives, one_axis_at_a_time(): return functools.reduce(lax.psum, axes, shard)  40.4 us
    all_to_all x1, blocking collectives, sent_and_summed(): blocks = lax.all_to_all(split_up(shard, dim, size), axis, 0, 0, tiled=True)  38.6 us
    all_gather x1, waiting for transfers between devices, on_device(): lax.all_gather(normed, DP, axis=0, tiled=True)  30.1 us
    all_to_all x1, blocking collectives, on_device(): lax.all_to_all(query_grads, FEAT_AXES, split_axis=1, concat_axis=0, tiled...  29 us
    all_gather x1, waiting for transfers between devices, on_device(): gathered = lax.all_gather(build_grads, DP, axis=0, tiled=True)  27.5 us
  transfers between devices with their start and end apart: 3, of which 3 were waited for; matrix products, arithmetic and copies ran while one was open for 0% of the time, Pallas kernels for 0%

commit v1 on v0

--- a/solution.py
+++ b/solution.py
@@ -4,6 +4,7 @@
 from jax import lax
 from jax.sharding import Mesh
 from jax.sharding import PartitionSpec as P
+from jax.lax import psum
 
 FEAT = 131072
 FEAT_AXES = ("feat_0", "feat_1")
@@ -51,7 +52,7 @@
     build_count = gathered.shape[0]
     cross_part = contract_last(gathered, q_local)
     gram_part = contract_last(gathered, gathered)
-    gram_matrix, cross_sums = lax.psum((gram_part, cross_part), FEAT_AXES)
+    gram_matrix, cross_sums = psum(psum((gram_part, cross_part), "feat_0"), "feat_1")
     build_wide = build_grads.astype(jnp.float32)
     square_total = one_axis_at_a_time(jnp.sum(build_wide * build_wide), FEAT_DP)
     damping = 0.1 * square_total / (build_count * FEAT) + 1e-06

time: 713 us -> 767 us (1.076)
  waiting for transfers between devices: 181 us -> 233 us
    psum x1 -> x2, waiting for transfers between devices: 123 us -> 175 us  [the longest x1 103 us: on_device(): psum((gram_part, cross_part), 'feat_0')]
  transfers between devices with their start and end apart: 3 -> 4, of which waited for: 3 -> 4; matrix products, arithmetic and copies ran while one was open for 0% -> 0% of each run, Pallas kernels for 0% -> 0%
where the time goes in v1:
time: 767 us; the launch traced here: 759 us
  other arithmetic  263 us (34%)
  waiting for transfers between devices  233 us (30%)
  blocking collectives  126 us (16%)
  matrix products  77.9 us (10%)
  local copies, waits for them, and re-layouts  39.3 us (5%)
  between operations  19.6 us (3%)
    another operation x30, other arithmetic, on_device(): factor = jnp.linalg.cholesky(gram_matrix)  168 us
    psum x1, waiting for transfers between devices, on_device(): psum((gram_part, cross_part), 'feat_0')  103 us
    another operation x4, other arithmetic, on_device(): solved = jax.scipy.linalg.cho_solve((factor, True), cross_sums)  83.7 us
    psum x1, waiting for transfers between devices, on_device(): psum(psum((gram_part, cross_part), 'feat_0'), 'feat_1')  72.3 us
    psum x4, blocking collectives, one_axis_at_a_time(): return functools.reduce(lax.psum, axes, shard)  40.5 us
    all_to_all x1, blocking collectives, sent_and_summed(): blocks = lax.all_to_all(split_up(shard, dim, size), axis, 0, 0, tiled=True)  38.6 us
    all_gather x1, waiting for transfers between devices, on_device(): lax.all_gather(normed, DP, axis=0, tiled=True)  30.1 us
    all_to_all x1, blocking collectives, on_device(): lax.all_to_all(query_grads, FEAT_AXES, split_axis=1, concat_axis=0, tiled...  29 us
  transfers between devices with their start and end apart: 4, of which 4 were waited for; matrix products, arithmetic and copies ran while one was open for 0% of the time, Pallas kernels for 0%

profile of v1, /device:TPU:32, one launch (start us, length us, event | category | flops | bytes accessed | tf_op | source)
XLA Modules:
  0.0 759.4 jit_solution(10800764814481311799)
XLA Ops:
  7.3 29.0 %all_to_all.30 = bf16[2,32,4096]{2,0,1:T(2,128)(2,1)S(1)} all-to-all(bf16[2,32,4096]{2,0,1:T(2,128)(2,1)} %bitcast.141), channel_id=1, replica_groups=mesh['feat_0'=4,'feat_1'=8,'dp_0'=4,'dp_1'=2] {'feat_0','feat_1'}, dimensions={1} | all-to-all | bytes 1048576 | tf_op jit(solution)/shard_map/all_to_all | solution.py:50
  36.5 27.5 %all-gather.3.cloned.1.call-done = bf16[1024,4096]{1,0:T(8,128)(2,1)} async-done(((bf16[128,4096]{1,0:T(8,128)(2,1)}), bf16[1024,4096]{1,0:T(8,128)(2,1)}) %all-gather.3.cloned.1.call-update) | async-done | bytes 8388624 | tf_op jit(solution)/shard_map/all_gather | solution.py:51
  64.0 15.9 %fusion.97 = f32[1024,1024]{0,1:T(8,128)} fusion(bf16[1024,4096]{1,0:T(8,128)(2,1)} %all-gather.3.cloned.1.call-done), kind=kOutput, calls=%fused_computation.222 | convolution fusion | flops 8589934592 | bytes 12582912 | tf_op jit(solution)/shard_map/dot_general | solution.py:44
  79.9 3.4 fusion.98
  83.4 102.5 %all-reduce.8.cloned.1.call-done = (f32[1024,1024]{0,1:T(8,128)}, f32[1024,64]{0,1:T(8,128)}) async-done(((f32[1024,1024]{0,1:T(8,128)}, f32[1024,64]{0,1:T(8,128)}), (f32[1024,1024]{0,1:T(8,128)}, f32[1024,64]{0,1:T(8,128)})) %all-reduce.8.cloned.1.call-update) | async-done | bytes 4456464 | tf_op jit(solution)/shard_map/psum | solution.py:55
  187.1 9.2 %psum.58 = f32[]{:T(128)} all-reduce(f32[]{:T(128)} %multiply_reduce_fusion), channel_id=1, replica_groups=mesh['feat_0'=4,'feat_1'=8,'dp_0'=4,'dp_1'=2] {'feat_0'}, use_global_device_ids=true, to_apply=%region_3.0 | all-reduce | flops 1 | bytes 8 | tf_op jit(solution)/shard_map/psum | solution.py:17
  196.3 17.0 %psum.59 = f32[]{:T(128)} all-reduce(f32[]{:T(128)} %psum.58), channel_id=1, replica_groups=mesh['feat_0'=4,'feat_1'=8,'dp_0'=4,'dp_1'=2] {'feat_1'}, use_global_device_ids=true, to_apply=%region_4.0 | all-reduce | flops 1 | bytes 8 | tf_op jit(solution)/shard_map/psum | solution.py:17
  213.3 11.2 %psum.60 = f32[]{:T(128)} all-reduce(f32[]{:T(128)} %psum.59), channel_id=1, replica_groups=mesh['feat_0'=4,'feat_1'=8,'dp_0'=4,'dp_1'=2] {'dp_0'}, use_global_device_ids=true, to_apply=%region_5.0 | all-reduce | flops 1 | bytes 8 | tf_op jit(solution)/shard_map/psum | solution.py:17
  224.5 3.1 psum.61
  228.3 72.3 %all-reduce.6.cloned.1.call-done = (f32[1024,1024]{0,1:T(8,128)}, f32[1024,64]{0,1:T(8,128)}) async-done(((f32[1024,1024]{0,1:T(8,128)}, f32[1024,64]{0,1:T(8,128)}), (f32[1024,1024]{0,1:T(8,128)}, f32[1024,64]{0,1:T(8,128)})) %all-reduce.6.cloned.1.call-update) | async-done | bytes 4456464 | tf_op jit(solution)/shard_map/psum | solution.py:55
  300.6 4.8 select_add_fusion
  305.4 5.8 copy.44
  311.2 4.5 fusion
  315.6 2.0 copy-done.2
  317.6 11.7 %cholesky.222 = f32[128,128]{1,0:T(8,128)S(1)} custom-call(f32[128,128]{1,0:T(8,128)S(1)} %cholesky.577), custom_call_target="Cholesky" | custom-call | tf_op jit(solution)/shard_map/jit(cholesky)/cholesky | solution.py:60
  329.5 9.8 %custom-call.66 = f32[1,128,128]{1,2,0:T(8,128)S(1)} custom-call(f32[1,128,128]{2,1,0:T(8,128)S(1)} %get-tuple-element.52), custom_call_target="InvertDiagBlocksLowerTriangular" | custom-call | tf_op jit(solution)/shard_map/jit(cholesky)/cholesky | solution.py:60
  339.3 1.5 fusion.11
  341.0 1.6 convolution_subtract_fusion.1
  342.6 11.7 %cholesky.243 = f32[128,128]{1,0:T(8,128)S(1)} custom-call(f32[128,128]{1,0:T(8,128)S(1)} %cholesky.581), custom_call_target="Cholesky" | custom-call | tf_op jit(solution)/shard_map/jit(cholesky)/cholesky | solution.py:60
  354.6 9.8 %custom-call.67 = f32[1,128,128]{1,2,0:T(8,128)S(1)} custom-call(f32[1,128,128]{2,1,0:T(8,128)S(1)} %get-tuple-element.50), custom_call_target="InvertDiagBlocksLowerTriangular" | custom-call | tf_op jit(solution)/shard_map/jit(cholesky)/cholesky | solution.py:60
  365.6 1.9 copy-done.1
  367.5 2.4 convolution_subtract_fusion.2
  369.9 11.7 %cholesky.466 = f32[128,128]{1,0:T(8,128)S(1)} custom-call(f32[128,128]{1,0:T(8,128)S(1)} %cholesky.586), custom_call_target="Cholesky" | custom-call | tf_op jit(solution)/shard_map/jit(cholesky)/cholesky | solution.py:60
  382.4 9.8 %custom-call.68 = f32[1,128,128]{1,2,0:T(8,128)S(1)} custom-call(f32[1,128,128]{2,1,0:T(8,128)S(1)} %get-tuple-element.48), custom_call_target="InvertDiagBlocksLowerTriangular" | custom-call | tf_op jit(solution)/shard_map/jit(cholesky)/cholesky | solution.py:60
  392.2 1.2 convolution_dynamic-update-slice_fusion.1
  393.5 3.3 convolution_subtract_fusion.3
  396.8 11.7 %cholesky.485 = f32[128,128]{1,0:T(8,128)S(1)} custom-call(f32[128,128]{1,0:T(8,128)S(1)} %cholesky.591), custom_call_target="Cholesky" | custom-call | tf_op jit(solution)/shard_map/jit(cholesky)/cholesky | solution.py:60
  409.3 9.8 %custom-call.69 = f32[1,128,128]{1,2,0:T(8,128)S(1)} custom-call(f32[1,128,128]{2,1,0:T(8,128)S(1)} %get-tuple-element.46), custom_call_target="InvertDiagBlocksLowerTriangular" | custom-call | tf_op jit(solution)/shard_map/jit(cholesky)/cholesky | solution.py:60
  420.3 3.2 convolution_subtract_fusion.4
  423.4 12.1 %cholesky.504 = f32[128,128]{1,0:T(8,128)S(1)} custom-call(f32[128,128]{1,0:T(8,128)S(1)} %cholesky.596), custom_call_target="Cholesky" | custom-call | tf_op jit(solution)/shard_map/jit(cholesky)/cholesky | solution.py:60
  436.3 9.8 %custom-call.70 = f32[1,128,128]{1,2,0:T(8,128)S(1)} custom-call(f32[1,128,128]{2,1,0:T(8,128)S(1)} %get-tuple-element.44), custom_call_target="InvertDiagBlocksLowerTriangular" | custom-call | tf_op jit(solution)/shard_map/jit(cholesky)/cholesky | solution.py:60
  447.3 3.1 convolution_subtract_fusion.5
  450.4 11.7 %cholesky.524 = f32[128,128]{1,0:T(8,128)S(1)} custom-call(f32[128,128]{1,0:T(8,128)S(1)} %cholesky.601), custom_call_target="Cholesky" | custom-call | tf_op jit(solution)/shard_map/jit(cholesky)/cholesky | solution.py:60
  462.8 9.8 %custom-call.71 = f32[1,128,128]{1,2,0:T(8,128)S(1)} custom-call(f32[1,128,128]{2,1,0:T(8,128)S(1)} %get-tuple-element.42), custom_call_target="InvertDiagBlocksLowerTriangular" | custom-call | tf_op jit(solution)/shard_map/jit(cholesky)/cholesky | solution.py:60
  473.6 2.8 convolution_subtract_fusion.6
  476.5 11.7 %cholesky.544 = f32[128,128]{1,0:T(8,128)S(1)} custom-call(f32[128,128]{1,0:T(8,128)S(1)} %cholesky.606), custom_call_target="Cholesky" | custom-call | tf_op jit(solution)/shard_map/jit(cholesky)/cholesky | solution.py:60
  489.0 9.8 %custom-call.72 = f32[1,128,128]{1,2,0:T(8,128)S(1)} custom-call(f32[1,128,128]{2,1,0:T(8,128)S(1)} %get-tuple-element.40), custom_call_target="InvertDiagBlocksLowerTriangular" | custom-call | tf_op jit(solution)/shard_map/jit(cholesky)/cholesky | solution.py:60
  499.7 2.1 convolution_subtract_fusion.7
  501.8 11.7 %cholesky.562 = f32[128,128]{1,0:T(8,128)S(1)} custom-call(f32[128,128]{1,0:T(8,128)S(1)} %convolution_subtract_fusion.7), custom_call_target="Cholesky" | custom-call | tf_op jit(solution)/shard_map/jit(cholesky)/cholesky | solution.py:60
  523.7 4.9 select_select_fusion
  528.6 24.0 %while.1 = (s32[]{:T(128)}, f32[1024,1024]{0,1:T(8,128)}, s32[8,2]{0,1:T(2,128)S(1)}, f32[8,128,128]{2,1,0:T(8,128)S(1)}, s32[]{:T(128)}) while((s32[]{:T(128)}, f32[1024,1024]{0,1:T(8,128)}, s32[8,2]{0,1:T(2,128)S(1)}, f32[8,128,128]{2,1,0:T(8,128)S(1)}, s32[]{:T(128)}) %tuple.53), condition=%wide.while_cond, body=%wide.while_body.sunk | while | flops 2 | bytes 393329 | solution.py:61
  529.3 2.3 dynamic-slice.7
  532.3 2.3 dynamic-slice.7
  535.3 2.3 dynamic-slice.7
  538.3 2.3 dynamic-slice.7
  541.3 2.3 dynamic-slice.7
  544.3 2.3 dynamic-slice.7
  547.3 2.3 dynamic-slice.7
  550.3 2.2 dynamic-slice.7
  552.6 78.8 %custom-call.73 = f32[8,128,128]{1,2,0:T(8,128)S(1)} custom-call(f32[8,128,128]{2,1,0:T(8,128)S(1)} %get-tuple-element.12), custom_call_target="InvertDiagBlocksLowerTriangular" | custom-call | tf_op jit(solution)/shard_map/jit(_cho_solve)/triangular_solve | solution.py:61
  635.6 1.2 convolution_subtract_fusion.21
  637.0 1.3 convolution_subtract_fusion.20
  638.5 1.4 convolution_subtract_fusion.19
  640.1 1.4 convolution_subtract_fusion.12
  644.7 1.3 convolution_subtract_fusion.9
  646.3 1.4 convolution_subtract_fusion.18
  647.9 1.5 convolution_subtract_fusion.17
  649.7 1.5 convolution_subtract_fusion.16
  651.6 1.7 convolution_subtract_fusion.8
  653.6 5.2 fusion.2
  658.8 17.6 %all_to_all.31 = f32[32,1,64]{2,1,0:T(1,128)S(1)} all-to-all(f32[32,1,64]{2,1,0:T(1,128)S(1)} %broadcast_in_dim.4), channel_id=1, replica_groups=mesh['feat_0'=4,'feat_1'=8,'dp_0'=4,'dp_1'=2] {'feat_0','feat_1'}, dimensions={0} | all-to-all | bytes 16384 | tf_op jit(solution)/shard_map/all_to_all | solution.py:22
  677.4 30.1 %all-gather.5.cloned.1.call-done = bf16[512,4096]{1,0:T(8,128)(2,1)} async-done(((bf16[64,4096]{1,0:T(8,128)(2,1)}), bf16[512,4096]{1,0:T(8,128)(2,1)}) %all-gather.5.cloned.1.call-update) | async-done | bytes 4194320 | tf_op jit(solution)/shard_map/all_gather | solution.py:70
  707.5 5.8 fusion.99
  713.4 38.6 %all_to_all.32 = f32[32,16,512]{2,1,0:T(8,128)S(1)} all-to-all(f32[32,16,512]{2,1,0:T(8,128)S(1)} %bitcast.140), channel_id=1, replica_groups=mesh['feat_0'=4,'feat_1'=8,'dp_0'=4,'dp_1'=2] {'feat_0','feat_1'}, dimensions={0} | all-to-all | bytes 2097152 | tf_op jit(solution)/shard_map/all_to_all | solution.py:39
  (146 shorter events, 33.9 us)
Async XLA Ops:
  6.5 57.5 %all-gather.3.cloned.1.call-start = ((), (), s32[]{:S(2)}) async-start(), calls=%async_computation.3 | async-start | bytes 9437184 | tf_op jit(solution)/shard_map/all_gather | solution.py:51
  7.3 178.6 %all-reduce.8.cloned.1.call-start = ((), (), s32[]{:S(2)}) async-start(), calls=%async_computation.6 | async-start | bytes 8912896 | tf_op jit(solution)/shard_map/psum | solution.py:55
  64.0 15.9 %copy-start = (bf16[1024,4096]{1,0:T(8,128)(2,1)S(1)}, bf16[1024,4096]{1,0:T(8,128)(2,1)}, u32[]{:S(2)}) copy-start(bf16[1024,4096]{1,0:T(8,128)(2,1)} %all-gather.3.cloned.1.call-done) | copy-start | bytes 25165828
  83.3 102.7 %copy-start.3 = (bf16[128,4096]{1,0:T(8,128)(2,1)S(1)}, bf16[128,4096]{1,0:T(8,128)(2,1)}, u32[]{:S(2)}) copy-start(bf16[128,4096]{1,0:T(8,128)(2,1)} %param.4) | copy-start | bytes 3145732
  83.3 217.2 %all-reduce.6.cloned.1.call-start = ((), (), s32[]{:S(2)}) async-start(), calls=%async_computation.5 | async-start | bytes 8912896 | tf_op jit(solution)/shard_map/psum | solution.py:55
  185.9 521.6 %all-gather.5.cloned.1.call-start = ((), (), s32[]{:S(2)}) async-start(), calls=%async_computation.4 | async-start | bytes 4718592 | tf_op jit(solution)/shard_map/all_gather | solution.py:70
  315.6 2.0 copy-start.2
  365.5 2.0 copy-start.1
  523.7 107.7 %copy-start.4 = (f32[1024,64]{0,1:T(8,128)S(1)}, f32[1024,64]{0,1:T(8,128)}, u32[]{:S(2)}) copy-start(f32[1024,64]{0,1:T(8,128)} %get-tuple-element.34) | copy-start | bytes 786436
Sparse Core Ops, SparseCore 0:
  9.2 54.7 all-gather.2
  83.4 102.3 all-reduce.7
  188.3 112.1 all-reduce.5
  677.6 29.9 all-gather.4
